TPU v7x, 512 devices: a whole 4x4x16 slice. The times are simulated.
512 devices in a mesh: blk: 8 (over y, core), tiles: 64 (over z, x).
Axes of the slice: x: 4, y: 4, z: 16, core: 2. Of those that a mesh axis runs over, the one named last changes fastest.
Arguments:
- tensor_tiles: bfloat16 [8, 128, 64, 4096], P('blk', 'tiles'), may hold values from -6 to 6
- tile_iblock: int32 [8, 128], P('blk', 'tiles'), may hold values from 0 to 7
- tile_jslot: int32 [8, 128], P('blk', 'tiles'), may hold values from 0 to 1, as said below
- tile_kslot: int32 [8, 128], P('blk', 'tiles'), may hold values from 0 to 1, as said below
- block_jlist: int32 [8, 128], P('blk', 'tiles'), may hold values from 0 to 255, as said below
- block_klist: int32 [8, 128], P('blk', 'tiles'), may hold values from 0 to 63, as said below
- factor_b: bfloat16 [256, 64, 512], P(None, 'tiles'), may hold values from -0.5 to 0.5
- factor_c: bfloat16 [64, 64, 512], P(None, 'tiles'), may hold values from -0.75 to 0.75
Outputs:
- mttkrp: float32 [32768, 512], P(('blk', 'tiles'))
Inputs may be any that keep to these rules, and one draw needn't show every extreme that they name: `block_jlist`: the 2 entries of one device's list are distinct. `block_klist`: the 2 entries of one device's list are distinct. `tile_jslot`: one device's tiles use between 1 and 2 distinct positions, and all 2 on some device. `tile_kslot`: one device's tiles use between 1 and 2 distinct positions, and all 2 on some device.
All inputs are finite; a program needn't handle non-finite values.
Results may differ from a plain program's by a relative error of at most 0.011.
Values may be sent and summed in bfloat16 or wider, within the bound.
A program may use at most 64 MiB of HBM per device.

v0:
```python
import jax
import jax.numpy as jnp
from jax import lax
from jax.sharding import PartitionSpec as P


def outgoing(asked, local, width):
    peers = asked.shape[0] // width
    table = asked.reshape(peers, width).T
    return jnp.take(local, table, axis=0)


def tile_term(local_tiles, which, mode_two, mode_three):
    tile_block = lax.dynamic_index_in_dim(local_tiles, which, 0, keepdims=False)
    inner = tile_block.shape[0]
    across = mode_two.shape[0]
    depth = mode_three.shape[0]
    contracted = jnp.dot(
        tile_block.reshape(inner * across, depth), mode_three, preferred_element_type=jnp.float32
    )
    return jnp.sum(
        contracted.reshape(inner, across, -1) * mode_two.astype(jnp.float32)[None], axis=1
    )


def per_device(
    tensor_tiles, tile_iblock, tile_jslot, tile_kslot, block_jlist, block_klist, factor_b, factor_c
):
    local_tiles = tensor_tiles[0]
    slots_two = tile_jslot[0]
    slots_three = tile_kslot[0]
    count = local_tiles.shape[0]
    wanted_two = jnp.take(block_jlist[0], slots_two)
    wanted_three = jnp.take(block_klist[0], slots_three)
    asked_two, asked_three = (
        lax.all_gather(wanted_two, "tiles", axis=0, tiled=True),
        lax.all_gather(wanted_three, "tiles", axis=0, tiled=True),
    )
    recv_two, recv_three = (
        lax.all_to_all(
            outgoing(asked_two, factor_b, count), "tiles", split_axis=1, concat_axis=2, tiled=True
        ),
        lax.all_to_all(
            outgoing(asked_three, factor_c, count), "tiles", split_axis=1, concat_axis=2, tiled=True
        ),
    )
    pick_two = jnp.arange(count, dtype=jnp.int32)
    pick_three = jnp.arange(count, dtype=jnp.int32)
    rank = factor_b.shape[2]
    fetched_two = recv_two.reshape(count, -1, rank)
    fetched_three = recv_three.reshape(count, -1, rank)
    groups = lax.axis_size("blk")
    inner = local_tiles.shape[1]
    owners = tile_iblock[0]

    def accumulate(which, partial_value):
        mode_two = lax.dynamic_index_in_dim(fetched_two, pick_two[which], 0, keepdims=False)
        mode_three = lax.dynamic_index_in_dim(fetched_three, pick_three[which], 0, keepdims=False)
        term = tile_term(local_tiles, which, mode_two, mode_three)
        target = owners[which]
        current = lax.dynamic_index_in_dim(partial_value, target, 0, keepdims=False)
        return lax.dynamic_update_index_in_dim(partial_value, current + term, target, 0)

    partial_value = lax.fori_loop(
        0, count, accumulate, jnp.zeros((groups, inner, rank), jnp.float32)
    )
    rounded = lax.optimization_barrier(partial_value.astype(jnp.bfloat16)).astype(jnp.float32)
    return lax.psum_scatter(
        rounded.reshape(groups * inner, rank).astype(jnp.bfloat16),
        "blk",
        scatter_dimension=0,
        tiled=True,
    ).astype(jnp.float32)


def solution(mesh):
    placed = (
        P("blk", "tiles", None, None),
        P("blk", "tiles"),
        P("blk", "tiles"),
        P("blk", "tiles"),
        P("blk", "tiles"),
        P("blk", "tiles"),
        P(None, "tiles", None),
        P(None, "tiles", None),
    )
    return jax.shard_map(
        per_device, mesh=mesh, in_specs=placed, out_specs=P(("blk", "tiles"), None), check_vma=False
    )
```

profile of v0, /device:TPU:4, one launch (start us, length us, event | category | flops | bytes accessed | tf_op | source)
XLA Modules:
  0.0 147.8 jit_solution(16779231108427683180)
XLA Ops:
  6.5 0.0 copy-start
  6.5 0.0 copy-start.2
  6.5 0.0 copy-start.3
  6.5 0.0 copy-start.1
  6.5 0.7 compare_select_fusion.3
  7.3 0.7 compare_select_fusion.2
  7.9 1.3 dynamic-slice
  9.9 1.3 gather_fusion.2
  11.2 1.3 gather_fusion.3
  12.5 0.0 copy-done.2
  12.5 0.1 fusion.4
  12.5 0.0 copy-done.3
  12.5 0.1 fusion.5
  12.6 31.5 %all-reduce.2 = (s32[128]{0:T(128)S(1)}, s32[128]{0:T(128)S(1)}) all-reduce(s32[128]{0:T(128)S(1)} %fusion.4, s32[128]{0:T(128)S(1)} %fusion.5), channel_id=1, replica_groups=mesh['blk'=8,'tiles'=64] {'tiles'}, use_global_device_ids=true, to_apply=%add | all-reduce | flops 256 | bytes 2048
  44.1 0.1 reshape.69
  44.3 0.1 copy.17
  44.3 0.1 reshape.94
  44.4 0.0 copy-done.1
  44.4 0.9 gather_fusion
  45.3 0.9 broadcast_select_fusion.1
  46.2 10.3 %all-to-all-start = ((bf16[2,64,1,512]{3,0,2,1:T(2,128)(2,1)}), bf16[2,64,1,512]{3,0,2,1:T(2,128)(2,1)S(1)}, u32[]{:S(2)}, u32[]{:S(2)}) async-start(bf16[2,64,1,512]{3,0,2,1:T(2,128)(2,1)} %broadcast_select_fusion.1), calls=%async_computation | async-start | bytes 262144 | tf_op jit(solution)/shard_map/all_to_all | solution.py:43
  56.5 0.1 reshape.71
  56.6 0.1 copy.19
  56.7 0.1 reshape.104
  56.8 0.0 copy-done
  56.8 0.9 gather_fusion.1
  57.7 0.0 copy-start.4
  57.7 0.9 broadcast_select_fusion
  58.6 12.3 %all-to-all-done = bf16[2,64,1,512]{3,0,2,1:T(2,128)(2,1)S(1)} async-done(((bf16[2,64,1,512]{3,0,2,1:T(2,128)(2,1)}), bf16[2,64,1,512]{3,0,2,1:T(2,128)(2,1)S(1)}, u32[]{:S(2)}, u32[]{:S(2)}) %all-to-all-start) | async-done | bytes 131104 | tf_op jit(solution)/shard_map/all_to_all | solution.py:43
  70.8 6.3 %all-to-all-start.1 = ((bf16[2,64,1,512]{3,0,2,1:T(2,128)(2,1)}), bf16[2,64,1,512]{3,0,2,1:T(2,128)(2,1)S(1)}, u32[]{:S(2)}, u32[]{:S(2)}) async-start(bf16[2,64,1,512]{3,0,2,1:T(2,128)(2,1)} %broadcast_select_fusion), calls=%async_computation.1 | async-start | bytes 262144 | tf_op jit(solution)/shard_map/all_to_all | solution.py:40
  77.2 0.0 reduce-scatter.2.cloned.1.call-start
  77.2 14.5 %all-to-all-done.1 = bf16[2,64,1,512]{3,0,2,1:T(2,128)(2,1)S(1)} async-done(((bf16[2,64,1,512]{3,0,2,1:T(2,128)(2,1)}), bf16[2,64,1,512]{3,0,2,1:T(2,128)(2,1)S(1)}, u32[]{:S(2)}, u32[]{:S(2)}) %all-to-all-start.1) | async-done | bytes 131104 | tf_op jit(solution)/shard_map/all_to_all | solution.py:40
  91.7 0.1 broadcast_in_dim.33
  91.9 0.0 copy-done.4
  91.9 16.1 %while.14 = (s32[]{:T(128)}, f32[8,64,512]{2,1,0:T(8,128)S(1)}, s32[2]{0:T(128)S(1)}, bf16[2,64,4096]{2,1,0:T(8,128)(2,1)}, s32[2]{0:T(128)S(1)}, /*index=5*/bf1...) while((s32[]{:T(128)}, f32[8,64,512]{2,1,0:T(8,128)S(1)}, ...), condition=%wide.region_2.4_spmd, body=%wide.region_0.3_spmd.sunk | while | flops 272662528 | bytes 4063449 | solution.py:64
  91.9 0.6 dynamic_slice.71
  94.2 1.1 constant_dynamic-slice_fusion.2
  95.3 1.1 dot_general.7
  96.4 1.2 multiply_reduce_fusion.2
  97.6 0.6 dynamic_slice.70
  100.0 0.6 dynamic_slice.71
  102.2 1.1 constant_dynamic-slice_fusion.2
  103.3 1.1 dot_general.7
  104.5 1.2 multiply_reduce_fusion.2
  105.7 0.6 dynamic_slice.70
  108.0 0.9 convert_element_type.18
  108.9 0.0 reduce-scatter.2.cloned.1.call-update
  108.9 30.6 %reduce-scatter.2.cloned.1.call-done = bf16[64,512]{1,0:T(8,128)(2,1)} async-done(((bf16[512,512]{1,0:T(8,128)(2,1)}), bf16[64,512]{1,0:T(8,128)(2,1)}) %reduce-scatter.2.cloned.1.call-update) | async-done | bytes 65552 | tf_op jit(solution)/shard_map/reduce_scatter | solution.py:68
  139.5 1.5 %convert_element_type.20 = f32[64,512]{1,0:T(8,128)} convert(bf16[64,512]{1,0:T(8,128)(2,1)} %reduce-scatter.2.cloned.1.call-done) | non-fusion elementwise | flops 32768 | bytes 196608 | tf_op jit(solution)/shard_map/convert_element_type | solution.py:73
  (17 shorter events, 0.2 us)
Async XLA Ops:
  6.5 50.3 %copy-start = (bf16[256,1,512]{2,0,1:T(8,128)(2,1)S(1)}, bf16[256,1,512]{2,0,1:T(8,128)(2,1)}, u32[]{:S(2)}) copy-start(bf16[256,1,512]{2,0,1:T(8,128)(2,1)} %param.18) | copy-start | bytes 786436
  6.5 5.9 %copy-start.2 = (s32[1,2]{1,0:T(1,128)S(1)}, s32[1,2]{1,0:T(1,128)}, u32[]{:S(2)}) copy-start(s32[1,2]{1,0:T(1,128)} %param.15) | copy-start | bytes 28
  6.5 6.0 %copy-start.3 = (s32[1,2]{1,0:T(1,128)S(1)}, s32[1,2]{1,0:T(1,128)}, u32[]{:S(2)}) copy-start(s32[1,2]{1,0:T(1,128)} %param.14) | copy-start | bytes 28
  6.5 37.9 %copy-start.1 = (bf16[64,1,512]{2,0,1:T(8,128)(2,1)S(1)}, bf16[64,1,512]{2,0,1:T(8,128)(2,1)}, u32[]{:S(2)}) copy-start(bf16[64,1,512]{2,0,1:T(8,128)(2,1)} %param.19) | copy-start | bytes 196612
  46.2 24.7 %all-to-all-start = ((bf16[2,64,1,512]{3,0,2,1:T(2,128)(2,1)}), bf16[2,64,1,512]{3,0,2,1:T(2,128)(2,1)S(1)}, u32[]{:S(2)}, u32[]{:S(2)}) async-start(bf16[2,64,1,512]{3,0,2,1:T(2,128)(2,1)} %broadcast_select_fusion.1), calls=%async_computation | async-start | bytes 262144 | tf_op jit(solution)/shard_map/all_to_all | solution.py:43
  57.7 34.2 %copy-start.4 = (s32[1,2]{1,0:T(1,128)S(1)}, s32[1,2]{1,0:T(1,128)}, u32[]{:S(2)}) copy-start(s32[1,2]{1,0:T(1,128)} %param.13) | copy-start | bytes 28
  70.8 20.9 %all-to-all-start.1 = ((bf16[2,64,1,512]{3,0,2,1:T(2,128)(2,1)}), bf16[2,64,1,512]{3,0,2,1:T(2,128)(2,1)S(1)}, u32[]{:S(2)}, u32[]{:S(2)}) async-start(bf16[2,64,1,512]{3,0,2,1:T(2,128)(2,1)} %broadcast_select_fusion), calls=%async_computation.1 | async-start | bytes 262144 | tf_op jit(solution)/shard_map/all_to_all | solution.py:40
  77.2 62.3 %reduce-scatter.2.cloned.1.call-start = ((), (), s32[]{:S(2)}) async-start(), calls=%async_computation.3 | async-start | bytes 589824 | tf_op jit(solution)/shard_map/reduce_scatter | solution.py:68
Sparse Core Ops, SparseCore 0:
  109.0 30.4 reduce-scatter.1
where the time goes:
time: 148 us
  waiting for transfers between devices  57.4 us (39%)
  blocking collectives  31.5 us (21%)
  starting transfers between devices  16.7 us (11%)
  between operations  14.2 us (10%)
  local copies, waits for them, and re-layouts  13 us (9%)
  loops' own time  6.83 us (5%)
  other arithmetic  5.82 us (4%)
  matrix products  2.48 us (2%)
    unnamed x1, blocking collectives  31.5 us
    reduce_scatter x1, waiting for transfers between devices, per_device(): lax.psum_scatter(rounded.reshape(groups * inner, rank).astype(jnp.bfloat1...  30.6 us
    all_to_all x1, waiting for transfers between devices, per_device(): lax.all_to_all(outgoing(asked_two, factor_b, count), 'tiles', split_axis=...  14.5 us
    all_to_all x1, waiting for transfers between devices, per_device(): lax.all_to_all(outgoing(asked_three, factor_c, count), 'tiles', split_axi...  12.3 us
    all_to_all x1, starting transfers between devices, per_device(): lax.all_to_all(outgoing(asked_three, factor_c, count), 'tiles', split_axi...  10.3 us
    another operation x1, loops' own time, per_device(): lax.fori_loop(0, count, accumulate, jnp.zeros((groups, inner, rank), jnp....  6.83 us
    all_to_all x1, starting transfers between devices, per_device(): lax.all_to_all(outgoing(asked_two, factor_b, count), 'tiles', split_axis=...  6.3 us
  transfers between devices with their start and end apart: 3, of which 3 were waited for; matrix products, arithmetic and copies ran while one was open for 1% of the time, Pallas kernels for 0%

commit v1 on v0

--- a/solution.py
+++ b/solution.py
@@ -40,8 +40,18 @@
         lax.all_to_all(
             outgoing(asked_two, factor_b, count), "tiles", split_axis=1, concat_axis=2, tiled=True
         ),
-        lax.all_to_all(
-            outgoing(asked_three, factor_c, count), "tiles", split_axis=1, concat_axis=2, tiled=True
+        jnp.concatenate(
+            jax.lax.all_to_all(
+                jnp.stack(
+                    jnp.split(
+                        outgoing(asked_three, factor_c, count), jax.lax.axis_size("tiles"), axis=1
+                    )
+                ),
+                "tiles",
+                0,
+                0,
+            ),
+            axis=2,
         ),
     )
     pick_two = jnp.arange(count, dtype=jnp.int32)

time: 148 us -> 187 us (1.26)
  the two profiles are of different devices: /device:TPU:4 before, /device:TPU:6 now
where the time goes in v1:
time: 187 us
  waiting for transfers between devices  57.7 us (31%)
  local copies, waits for them, and re-layouts  50.6 us (27%)
  blocking collectives  32.4 us (17%)
  starting transfers between devices  15.7 us (8%)
  between operations  14.2 us (8%)
  loops' own time  8.39 us (4%)
  other arithmetic  5.16 us (3%)
  matrix products  2.5 us (1%)
    unnamed x76, local copies, waits for them, and re-layouts  37.9 us
    unnamed x1, blocking collectives  32.4 us
    reduce_scatter x1, waiting for transfers between devices, per_device(): lax.psum_scatter(rounded.reshape(groups * inner, rank).astype(jnp.bfloat1...  30.6 us
    all_to_all x1, waiting for transfers between devices, per_device(): lax.all_to_all(outgoing(asked_two, factor_b, count), 'tiles', split_axis=...  14.5 us
    all_to_all x1, waiting for transfers between devices, per_device(): jax.lax.all_to_all(jnp.stack(jnp.split(outgoing(asked_three, factor_c, co...  12.6 us
    all_to_all x1, starting transfers between devices, per_device(): jax.lax.all_to_all(jnp.stack(jnp.split(outgoing(asked_three, factor_c, co...  9.39 us
    another operation x1, loops' own time, per_device(): lax.fori_loop(0, count, accumulate, jnp.zeros((groups, inner, rank), jnp....  8.39 us
    all_to_all x1, starting transfers between devices, per_device(): lax.all_to_all(outgoing(asked_two, factor_b, count), 'tiles', split_axis=...  6.29 us
  transfers between devices with their start and end apart: 3, of which 3 were waited for; matrix products, arithmetic and copies ran while one was open for 1% of the time, Pallas kernels for 0%

profile of v1, /device:TPU:6, one launch (start us, length us, event | category | flops | bytes accessed | tf_op | source)
XLA Modules:
  0.0 186.6 jit_solution(441126362347631427)
XLA Ops:
  6.5 0.7 compare_select_fusion.3
  7.3 0.7 compare_select_fusion.2
  7.9 1.3 dynamic-slice
  9.9 1.3 gather_fusion.2
  11.2 1.3 gather_fusion.3
  12.6 32.4 %all-reduce.2 = (s32[128]{0:T(128)S(1)}, s32[128]{0:T(128)S(1)}) all-reduce(s32[128]{0:T(128)S(1)} %fusion.4, s32[128]{0:T(128)S(1)} %fusion.5), channel_id=1, replica_groups=mesh['blk'=8,'tiles'=64] {'tiles'}, use_global_device_ids=true, to_apply=%add | all-reduce | flops 256 | bytes 2048
  45.7 0.9 gather_fusion
  46.7 0.6 constant_dynamic-update-slice_fusion.63
  47.3 0.6 constant_dynamic-update-slice_fusion.62
  47.9 0.6 constant_dynamic-update-slice_fusion.61
  48.5 0.6 constant_dynamic-update-slice_fusion.60
  53.1 0.6 constant_dynamic-update-slice_fusion.52
  53.7 0.6 constant_dynamic-update-slice_fusion.51
  54.3 0.6 constant_dynamic-update-slice_fusion.50
  54.9 0.6 constant_dynamic-update-slice_fusion.49
  55.5 0.6 constant_dynamic-update-slice_fusion.48
  56.0 0.6 constant_dynamic-update-slice_fusion.47
  56.6 0.6 constant_dynamic-update-slice_fusion.46
  57.2 0.6 constant_dynamic-update-slice_fusion.45
  57.8 0.6 constant_dynamic-update-slice_fusion.44
  58.4 0.6 constant_dynamic-update-slice_fusion.43
  59.0 0.6 constant_dynamic-update-slice_fusion.42
  59.5 0.6 constant_dynamic-update-slice_fusion.41
  64.2 0.6 constant_dynamic-update-slice_fusion.33
  64.8 0.6 constant_dynamic-update-slice_fusion.32
  65.3 0.6 constant_dynamic-update-slice_fusion.31
  65.9 0.6 constant_dynamic-update-slice_fusion.30
  66.5 0.6 constant_dynamic-update-slice_fusion.29
  67.1 0.6 constant_dynamic-update-slice_fusion.28
  67.7 0.6 constant_dynamic-update-slice_fusion.27
  68.3 0.6 constant_dynamic-update-slice_fusion.26
  68.8 0.6 constant_dynamic-update-slice_fusion.25
  69.4 0.6 constant_dynamic-update-slice_fusion.24
  70.0 0.6 constant_dynamic-update-slice_fusion.23
  70.6 0.6 constant_dynamic-update-slice_fusion.22
  75.2 0.6 constant_dynamic-update-slice_fusion.14
  75.8 0.6 constant_dynamic-update-slice_fusion.13
  76.4 0.6 constant_dynamic-update-slice_fusion.12
  77.0 0.6 constant_dynamic-update-slice_fusion.11
  77.6 0.6 constant_dynamic-update-slice_fusion.10
  78.1 0.6 constant_dynamic-update-slice_fusion.9
  78.7 0.6 constant_dynamic-update-slice_fusion.8
  79.3 0.6 constant_dynamic-update-slice_fusion.7
  79.9 0.6 constant_dynamic-update-slice_fusion.6
  84.0 9.4 %all-to-all-start = ((bf16[64,2,1,1,512]{4,1,3,2,0:T(2,128)(2,1)}), bf16[64,2,1,1,512]{4,1,3,2,0:T(2,128)(2,1)S(1)}, u32[]{:S(2)}, u32[]{:S(2)}) async-start(bf16[64,2,1,1,512]{4,1,3,2,0:T(2,128)(2,1)} %constant_dynamic-update-slice_fusion), calls=%async_computation | async-start | bytes 262144 | tf_op jit(solution)/shard_map/all_to_all | solution.py:44
  93.4 0.8 gather_fusion.1
  94.2 0.9 broadcast_select_fusion
  95.1 12.6 %all-to-all-done = bf16[64,2,1,1,512]{4,1,3,2,0:T(2,128)(2,1)S(1)} async-done(((bf16[64,2,1,1,512]{4,1,3,2,0:T(2,128)(2,1)}), bf16[64,2,1,1,512]{4,1,3,2,0:T(2,128)(2,1)S(1)}, u32[]{:S(2)}, u32[]{:S(2)}) %all-to-all-start) | async-done | bytes 131104 | tf_op jit(solution)/shard_map/all_to_all | solution.py:44
  107.7 6.3 %all-to-all-start.1 = ((bf16[2,64,1,512]{3,0,2,1:T(2,128)(2,1)}), bf16[2,64,1,512]{3,0,2,1:T(2,128)(2,1)S(1)}, u32[]{:S(2)}, u32[]{:S(2)}) async-start(bf16[2,64,1,512]{3,0,2,1:T(2,128)(2,1)} %broadcast_select_fusion), calls=%async_computation.1 | async-start | bytes 262144 | tf_op jit(solution)/shard_map/all_to_all | solution.py:40
  114.1 14.5 %all-to-all-done.1 = bf16[2,64,1,512]{3,0,2,1:T(2,128)(2,1)S(1)} async-done(((bf16[2,64,1,512]{3,0,2,1:T(2,128)(2,1)}), bf16[2,64,1,512]{3,0,2,1:T(2,128)(2,1)S(1)}, u32[]{:S(2)}, u32[]{:S(2)}) %all-to-all-start.1) | async-done | bytes 131104 | tf_op jit(solution)/shard_map/all_to_all | solution.py:40
  128.7 18.1 %while.14 = (s32[]{:T(128)}, f32[8,64,512]{2,1,0:T(8,128)S(1)}, s32[2]{0:T(128)S(1)}, bf16[2,64,4096]{2,1,0:T(8,128)(2,1)}, s32[2]{0:T(128)S(1)}, /*index=5*/bf1...) while((s32[]{:T(128)}, f32[8,64,512]{2,1,0:T(8,128)S(1)}, ...), condition=%wide.region_2.4_spmd, body=%wide.region_0.3_spmd.sunk | while | flops 272662528 | bytes 4063449 | solution.py:74
  128.7 0.7 dynamic_slice.71
  131.5 1.1 constant_dynamic-slice_fusion.2
  132.6 1.1 dot_general.7
  133.7 1.2 multiply_reduce_fusion.2
  135.0 0.7 dynamic_slice.70
  137.8 0.7 dynamic_slice.71
  140.5 1.1 constant_dynamic-slice_fusion.2
  141.6 1.1 dot_general.7
  142.7 1.3 multiply_reduce_fusion.2
  144.0 0.7 dynamic_slice.70
  146.8 0.9 convert_element_type.18
  147.7 30.6 %reduce-scatter.2.cloned.1.call-done = bf16[64,512]{1,0:T(8,128)(2,1)} async-done(((bf16[512,512]{1,0:T(8,128)(2,1)}), bf16[64,512]{1,0:T(8,128)(2,1)}) %reduce-scatter.2.cloned.1.call-update) | async-done | bytes 65552 | tf_op jit(solution)/shard_map/reduce_scatter | solution.py:78
  178.3 1.5 convert_element_type.20
  (65 shorter events, 17.0 us)
Async XLA Ops:
  6.5 86.8 %copy-start = (bf16[256,1,512]{2,0,1:T(8,128)(2,1)S(1)}, bf16[256,1,512]{2,0,1:T(8,128)(2,1)}, u32[]{:S(2)}) copy-start(bf16[256,1,512]{2,0,1:T(8,128)(2,1)} %param.18) | copy-start | bytes 786436
  6.5 5.9 %copy-start.2 = (s32[1,2]{1,0:T(1,128)S(1)}, s32[1,2]{1,0:T(1,128)}, u32[]{:S(2)}) copy-start(s32[1,2]{1,0:T(1,128)} %param.15) | copy-start | bytes 28
  6.5 6.0 %copy-start.3 = (s32[1,2]{1,0:T(1,128)S(1)}, s32[1,2]{1,0:T(1,128)}, u32[]{:S(2)}) copy-start(s32[1,2]{1,0:T(1,128)} %param.14) | copy-start | bytes 28
  6.5 39.1 %copy-start.1 = (bf16[64,1,512]{2,0,1:T(8,128)(2,1)S(1)}, bf16[64,1,512]{2,0,1:T(8,128)(2,1)}, u32[]{:S(2)}) copy-start(bf16[64,1,512]{2,0,1:T(8,128)(2,1)} %param.19) | copy-start | bytes 196612
  84.0 23.8 %all-to-all-start = ((bf16[64,2,1,1,512]{4,1,3,2,0:T(2,128)(2,1)}), bf16[64,2,1,1,512]{4,1,3,2,0:T(2,128)(2,1)S(1)}, u32[]{:S(2)}, u32[]{:S(2)}) async-start(bf16[64,2,1,1,512]{4,1,3,2,0:T(2,128)(2,1)} %constant_dynamic-update-slice_fusion), calls=%async_computation | async-start | bytes 262144 | tf_op jit(solution)/shard_map/all_to_all | solution.py:44
  94.2 34.5 %copy-start.4 = (s32[1,2]{1,0:T(1,128)S(1)}, s32[1,2]{1,0:T(1,128)}, u32[]{:S(2)}) copy-start(s32[1,2]{1,0:T(1,128)} %param.13) | copy-start | bytes 28
  107.7 20.8 %all-to-all-start.1 = ((bf16[2,64,1,512]{3,0,2,1:T(2,128)(2,1)}), bf16[2,64,1,512]{3,0,2,1:T(2,128)(2,1)S(1)}, u32[]{:S(2)}, u32[]{:S(2)}) async-start(bf16[2,64,1,512]{3,0,2,1:T(2,128)(2,1)} %broadcast_select_fusion), calls=%async_computation.1 | async-start | bytes 262144 | tf_op jit(solution)/shard_map/all_to_all | solution.py:40
  114.0 64.3 %reduce-scatter.2.cloned.1.call-start = ((), (), s32[]{:S(2)}) async-start(), calls=%async_computation.3 | async-start | bytes 589824 | tf_op jit(solution)/shard_map/reduce_scatter | solution.py:78
Sparse Core Ops, SparseCore 0:
  147.8 30.4 reduce-scatter.1
